TPU v7x, 128 devices: a whole 4x4x4 slice. The times are simulated.
128 devices in a mesh: row: 16 (over z, x), mp: 8 (over y, core).
Axes of the slice: x: 4, y: 4, z: 4, core: 2. Of those that a mesh axis runs over, the one named last changes fastest.
Arguments:
- token_ids: int32 [128, 128], P('row'), may hold values from 0 to 511
- set_lengths: int32 [128], P('row'), may hold values from 32 to 128
- live_counts: int32 [16], replicated, may hold values from 1 to 8, 64 in all
- embed_table: bfloat16 [512, 5120], replicated, may hold values from -3 to 3
- position_table: bfloat16 [128, 5120], replicated, may hold values from -3 to 3
- norm_gain: float32 [5120], replicated, may hold values from 0.1 to 1.9
- w_query: bfloat16 [5120, 5120], P('row', 'mp')
- w_key: bfloat16 [5120, 5120], P('row', 'mp')
- w_value: bfloat16 [5120, 5120], P('row', 'mp'), may hold values from -0.078125 to 0.078125
- w_out: bfloat16 [5120, 5120], P('mp', 'row'), may hold values from -0.078125 to 0.078125
Outputs:
- verified: bfloat16 [128, 128, 5120], P('row', None, 'mp')
Inputs may be any that keep to these rules, and one draw needn't show every extreme that they name: Owner group g has live_counts[g] live sets, its first slots; the counts sum to 64 and one group holds 8. `set_lengths`: positions at or past a set's length are padding.
All inputs are finite; a program needn't handle non-finite values.
Results may differ from a plain program's by a relative error of at most 0.017.
Values may be sent and summed in bfloat16 or wider, within the bound.
No kernel may reach another device: no remote copies, remote signals or barrier semaphores. Data moves between devices by JAX's collectives and lax.ppermute only.
A program may use at most 128 MiB of HBM per device.

v0:
```python
import jax
import jax.numpy as jnp
from jax import lax
from jax.sharding import PartitionSpec as P

DH = 128


def prepare(group_ids, embed_table, position_table, norm_gain):
    summed = (
        jnp.take(embed_table, group_ids, axis=0).astype(jnp.float32)
        + position_table.astype(jnp.float32)[None]
    )
    stored = lax.optimization_barrier(summed.astype(jnp.bfloat16))
    widened = stored.astype(jnp.float32)
    inverse = lax.rsqrt(jnp.mean(widened * widened, axis=-1, keepdims=True) + 1e-05)
    normed = (widened * inverse * norm_gain).astype(jnp.bfloat16)
    return (stored, normed)


def attend(query, keys, values, group_lengths):
    set_count = group_lengths.shape[0]
    seq_len = query.shape[0] // set_count
    q_four = query.reshape(set_count, seq_len, -1, DH)
    k_four = keys.reshape(set_count, seq_len, -1, DH)
    v_four = values.reshape(set_count, seq_len, -1, DH)
    scores = jnp.einsum(
        "sqhd,skhd->shqk", q_four, k_four, preferred_element_type=jnp.float32
    ) * DH ** (-0.5)
    valid = jnp.arange(seq_len)[None, :] < group_lengths[:, None]
    scores = jnp.where(valid[:, None, None, :], scores, -1e30)
    highest = jnp.max(scores, axis=-1, keepdims=True)
    expo = jnp.exp(scores - highest)
    weights = (expo / jnp.sum(expo, axis=-1, keepdims=True)).astype(jnp.bfloat16)
    mixed = jnp.einsum("shqk,skhd->sqhd", weights, v_four, preferred_element_type=jnp.float32)
    return mixed.astype(jnp.bfloat16).reshape(set_count * seq_len, -1)


def verify(
    group_ids,
    group_lengths,
    live,
    embed_table,
    position_table,
    norm_gain,
    w_query,
    w_key,
    w_value,
    w_out,
):
    set_count, seq_len = group_ids.shape
    stored, normed = prepare(group_ids, embed_table, position_table, norm_gain)
    flat = normed.reshape(set_count * seq_len, -1)
    query = jnp.dot(
        flat, lax.all_gather(w_query, "row", axis=0, tiled=True), preferred_element_type=jnp.float32
    )
    keys = jnp.dot(
        flat, lax.all_gather(w_key, "row", axis=0, tiled=True), preferred_element_type=jnp.float32
    )
    values = jnp.dot(
        flat, lax.all_gather(w_value, "row", axis=0, tiled=True), preferred_element_type=jnp.float32
    )
    mixed = attend(
        query.astype(jnp.bfloat16),
        keys.astype(jnp.bfloat16),
        values.astype(jnp.bfloat16),
        group_lengths,
    )
    partial_value = jnp.dot(
        mixed, lax.all_gather(w_out, "row", axis=1, tiled=True), preferred_element_type=jnp.float32
    )
    summed = lax.psum_scatter(
        partial_value.astype(jnp.bfloat16), "mp", scatter_dimension=1, tiled=True
    ).astype(jnp.float32)
    features = summed.shape[1]
    residual = lax.dynamic_slice_in_dim(
        stored.reshape(set_count * seq_len, -1), lax.axis_index("mp") * features, features, 1
    )
    valid = jnp.arange(seq_len)[None, :] < group_lengths[:, None]
    keep = (live[:, None] & valid).reshape(-1, 1).astype(jnp.float32)
    output = ((residual.astype(jnp.float32) + summed) * keep).astype(jnp.bfloat16)
    return output.reshape(set_count, seq_len, features)


def on_device(
    token_ids,
    set_lengths,
    live_counts,
    embed_table,
    position_table,
    norm_gain,
    w_query,
    w_key,
    w_value,
    w_out,
):
    slot_count, seq_len = token_ids.shape
    my_group = lax.axis_index("row")
    own_live = jnp.arange(slot_count) < live_counts[my_group]
    return verify(
        token_ids,
        set_lengths,
        own_live,
        embed_table,
        position_table,
        norm_gain,
        w_query,
        w_key,
        w_value,
        w_out,
    )


def solution(mesh):
    in_specs = (
        P("row", None),
        P("row"),
        P(),
        P(),
        P(),
        P(),
        P("row", "mp"),
        P("row", "mp"),
        P("row", "mp"),
        P("mp", "row"),
    )
    out_specs = P("row", None, "mp")
    return jax.shard_map(
        on_device, mesh=mesh, in_specs=in_specs, out_specs=out_specs, check_vma=False
    )
```

profile of v0, /device:TPU:1, one launch (start us, length us, event | category | flops | bytes accessed | tf_op | source)
XLA Modules:
  0.0 368.8 jit_solution(6773406523633156874)
XLA Ops:
  6.5 0.7 all-gather.7.cloned.1.call-update
  7.3 0.7 all-gather.9.cloned.1.call-update
  8.1 0.7 all-gather.5.cloned.1.call-update
  8.8 0.5 all-gather.11.cloned.1.call-update
  9.4 1.6 convert_element_type.57
  11.0 21.7 %gather_fusion = bf16[1024,5120]{1,0:T(8,128)(2,1)} fusion(bf16[512,5120]{1,0:T(8,128)(2,1)} %param.13, s32[1024]{0:T(1024)S(1)} %bitcast_clamp_fusion), kind=kCustom, calls=%fused_computation | custom fusion | bytes 20975616 | tf_op jit(solution)/shard_map/jit(_take)/gather | solution.py:11
  32.7 11.0 %add_convert_fusion = bf16[8,128,5120]{2,1,0:T(8,128)(2,1)} fusion(f32[128,5120]{1,0:T(8,128)S(1)} %convert_element_type.57, bf16[8,128,5120]{2,1,0:T(8,128)(2,1)} %bitcast.28, pred[8,128]{1,0:T(8,128)(4,1)S(1)} %compare_and_fusion), kind=kLoop, calls=%fused_computation.7 | loop fusion | flops 20971520 | bytes 23593984 | tf_op jit(solution)/shard_map/convert_element_type | solution.py:14
  43.7 0.6 dynamic_slice.7
  44.3 0.6 iota_compare_fusion.1
  45.0 6.5 %fusion.1 = f32[8,128]{1,0:T(8,128)S(1)} fusion(bf16[8,128,5120]{2,1,0:T(8,128)(2,1)} %add_convert_fusion), kind=kLoop, calls=%fused_computation.4 | loop fusion | flops 15727616 | bytes 10489856 | tf_op jit(solution)/shard_map/reduce_sum | solution.py:16
  51.5 0.8 copy-done
  52.4 5.9 %fusion.3 = bf16[8,128,5120]{2,1,0:T(8,128)(2,1)} fusion(bf16[8,128,5120]{2,1,0:T(8,128)(2,1)S(1)} %copy-done, f32[5120]{0:T(1024)S(1)} %copy-done.3, f32[8,128]{1,0:T(8,128)S(1)} %add_rsqrt_fusion), kind=kLoop, calls=%fused_computation.6 | loop fusion | flops 20971520 | bytes 20996096 | tf_op jit(solution)/shard_map/convert_element_type | solution.py:17
  58.3 17.0 %all-gather.7.cloned.1.call-done = bf16[5120,640]{1,0:T(8,128)(2,1)} async-done(((bf16[320,640]{1,0:T(8,128)(2,1)}), bf16[5120,640]{1,0:T(8,128)(2,1)}) %all-gather.7.cloned.1.call-update) | async-done | bytes 6553616 | tf_op jit(solution)/shard_map/all_gather | solution.py:55
  75.3 12.9 %convolution_convert_fusion.3 = bf16[1024,640]{1,0:T(8,128)(2,1)S(1)} fusion(bf16[1024,5120]{1,0:T(8,128)(2,1)} %bitcast.30, bf16[5120,640]{1,0:T(8,128)(2,1)} %all-gather.7.cloned.1.call-done), kind=kOutput, calls=%fused_computation.16 | convolution fusion | flops 6711541760 | bytes 18350080 | tf_op jit(solution)/shard_map/dot_general | solution.py:54
  88.2 1.5 reshape.103
  89.7 49.9 %all-gather.9.cloned.1.call-done = bf16[5120,640]{1,0:T(8,128)(2,1)} async-done(((bf16[320,640]{1,0:T(8,128)(2,1)}), bf16[5120,640]{1,0:T(8,128)(2,1)}) %all-gather.9.cloned.1.call-update) | async-done | bytes 6553616 | tf_op jit(solution)/shard_map/all_gather | solution.py:58
  139.6 12.9 %convolution_convert_fusion.2 = bf16[1024,640]{1,0:T(8,128)(2,1)S(1)} fusion(bf16[1024,5120]{1,0:T(8,128)(2,1)} %bitcast.31, bf16[5120,640]{1,0:T(8,128)(2,1)} %all-gather.9.cloned.1.call-done), kind=kOutput, calls=%fused_computation.15 | convolution fusion | flops 6711541760 | bytes 18350080 | tf_op jit(solution)/shard_map/dot_general | solution.py:57
  152.5 2.5 reshape.104
  154.9 48.9 %all-gather.5.cloned.1.call-done = bf16[5120,640]{1,0:T(8,128)(2,1)} async-done(((bf16[320,640]{1,0:T(8,128)(2,1)}), bf16[5120,640]{1,0:T(8,128)(2,1)}) %all-gather.5.cloned.1.call-update) | async-done | bytes 6553616 | tf_op jit(solution)/shard_map/all_gather | solution.py:61
  203.9 12.9 %convolution_convert_fusion.4 = bf16[1024,640]{1,0:T(8,128)(2,1)S(1)} fusion(bf16[1024,5120]{1,0:T(8,128)(2,1)} %bitcast.32, bf16[5120,640]{1,0:T(8,128)(2,1)} %all-gather.5.cloned.1.call-done), kind=kOutput, calls=%fused_computation.17 | convolution fusion | flops 6711541760 | bytes 18350080 | tf_op jit(solution)/shard_map/dot_general | solution.py:60
  216.8 2.5 reshape.102
  219.3 2.6 fusion.8
  221.9 1.5 copy-done.1
  223.4 0.8 fusion.23
  224.4 3.1 fusion.5
  227.5 0.9 copy.30
  228.4 39.6 %all-gather.11.cloned.1.call-done = bf16[640,5120]{0,1:T(8,128)(2,1)} async-done(((bf16[640,320]{0,1:T(8,128)(2,1)}), bf16[640,5120]{0,1:T(8,128)(2,1)}) %all-gather.11.cloned.1.call-update) | async-done | bytes 6553616 | tf_op jit(solution)/shard_map/all_gather | solution.py:70
  268.0 13.7 %convolution_convert_fusion = bf16[1024,5120]{1,0:T(8,128)(2,1)} fusion(bf16[640,5120]{0,1:T(8,128)(2,1)} %all-gather.11.cloned.1.call-done, bf16[80,8,8,128]{3,2,1,0:T(8,128)(2,1)S(1)} %bitcast.34), kind=kOutput, calls=%fused_computation.8 | convolution fusion | flops 6716129280 | bytes 18350080 | tf_op jit(solution)/shard_map/dot_general | solution.py:69
  281.7 14.4 %copy.38 = bf16[1024,5120]{0,1:T(8,128)(2,1)} copy(bf16[1024,5120]{1,0:T(8,128)(2,1)} %convolution_convert_fusion) | data formatting | bytes 20971520
  296.2 61.6 %reduce-scatter.4.cloned.1.call-done = bf16[640,1024]{1,0:T(8,128)(2,1)} async-done(((bf16[5120,1024]{1,0:T(8,128)(2,1)}), bf16[640,1024]{1,0:T(8,128)(2,1)}) %reduce-scatter.4.cloned.1.call-update) | async-done | bytes 1310736
  357.7 1.7 copy.39
  359.4 2.8 multiply_convert_fusion
  (22 shorter events, 0.5 us)
Async XLA Ops:
  6.5 68.7 %all-gather.7.cloned.1.call-start = ((), (), s32[]{:S(2)}) async-start(), calls=%async_computation.2 | async-start | bytes 6963200 | tf_op jit(solution)/shard_map/all_gather | solution.py:55
  7.3 3.7 %copy-start.4 = (s32[8,128]{1,0:T(8,128)S(1)}, s32[8,128]{1,0:T(8,128)}, u32[]{:S(2)}) copy-start(s32[8,128]{1,0:T(8,128)} %param.10) | copy-start | bytes 12292
  7.3 132.3 %all-gather.9.cloned.1.call-start = ((), (), s32[]{:S(2)}) async-start(), calls=%async_computation.3 | async-start | bytes 6963200 | tf_op jit(solution)/shard_map/all_gather | solution.py:58
  8.0 195.8 %all-gather.5.cloned.1.call-start = ((), (), s32[]{:S(2)}) async-start(), calls=%async_computation.1 | async-start | bytes 6963200 | tf_op jit(solution)/shard_map/all_gather | solution.py:61
  8.8 259.3 %all-gather.11.cloned.1.call-start = ((), (), s32[]{:S(2)}) async-start(), calls=%async_computation.4 | async-start | bytes 6963200 | tf_op jit(solution)/shard_map/all_gather | solution.py:70
  9.3 348.4 %reduce-scatter.4.cloned.1.call-start = ((), (), s32[]{:S(2)}) async-start(), calls=%async_computation.5 | async-start | bytes 11796480
  32.7 11.0 %copy-start.6 = (s32[16]{0:T(128)S(1)}, s32[16]{0:T(128)}, u32[]{:S(2)}) copy-start(s32[16]{0:T(128)} %param.12) | copy-start | bytes 196
  32.7 12.2 %copy-start.5 = (s32[8]{0:T(128)S(1)}, s32[8]{0:T(128)}, u32[]{:S(2)}) copy-start(s32[8]{0:T(128)} %param.11) | copy-start | bytes 100
  32.7 18.8 %copy-start.3 = (f32[5120]{0:T(1024)S(1)}, f32[5120]{0:T(1024)}, u32[]{:S(2)}) copy-start(f32[5120]{0:T(1024)} %param.15) | copy-start | bytes 61444
  45.0 7.4 %copy-start = (bf16[8,128,5120]{2,1,0:T(8,128)(2,1)S(1)}, bf16[8,128,5120]{2,1,0:T(8,128)(2,1)}, u32[]{:S(2)}) copy-start(bf16[8,128,5120]{2,1,0:T(8,128)(2,1)} %add_convert_fusion) | copy-start | bytes 31457284
  221.9 1.5 copy-start.1
  221.9 2.5 copy-start.2
Sparse Core Ops, SparseCore 0:
  9.5 65.7 all-gather.6
  77.4 62.1 all-gather.8
  141.7 62.1 all-gather.4
  205.8 62.1 all-gather.10
  296.3 61.4 reduce-scatter.3
where the time goes:
time: 370 us; the launch traced here: 369 us
  waiting for transfers between devices  220 us (59%)
  matrix products  58.1 us (16%)
  local copies, waits for them, and re-layouts  48.2 us (13%)
  other arithmetic  29.3 us (8%)
  between operations  13.3 us (4%)
    unnamed x6, waiting for transfers between devices  64.2 us
    all_gather x1, waiting for transfers between devices, verify(): lax.all_gather(w_key, 'row', axis=0, tiled=True)  49.9 us
    all_gather x1, waiting for transfers between devices, verify(): lax.all_gather(w_value, 'row', axis=0, tiled=True)  48.9 us
    all_gather x1, waiting for transfers between devices, verify(): lax.all_gather(w_out, 'row', axis=1, tiled=True)  39.6 us
    gather x1, local copies, waits for them, and re-layouts, prepare(): jnp.take(embed_table, group_ids, axis=0).astype(jnp.float32)  21.7 us
    unnamed x16, local copies, waits for them, and re-layouts  18.6 us
    all_gather x1, waiting for transfers between devices, verify(): lax.all_gather(w_query, 'row', axis=0, tiled=True)  17 us
    dot_general x1, matrix products, verify(): jnp.dot(mixed, lax.all_gather(w_out, 'row', axis=1, tiled=True), preferre...  13.7 us
  transfers between devices with their start and end apart: 5, of which 5 were waited for; matrix products, arithmetic and copies ran while one was open for 27% of the time, Pallas kernels for 0%

commit v1 on v0

--- a/solution.py
+++ b/solution.py
@@ -67,7 +67,11 @@
         group_lengths,
     )
     partial_value = jnp.dot(
-        mixed, lax.all_gather(w_out, "row", axis=1, tiled=True), preferred_element_type=jnp.float32
+        mixed,
+        jnp.concatenate(
+            lax.all_to_all(jnp.stack([w_out] * lax.axis_size("row")), "row", 0, 0), axis=1
+        ),
+        preferred_element_type=jnp.float32,
     )
     summed = lax.psum_scatter(
         partial_value.astype(jnp.bfloat16), "mp", scatter_dimension=1, tiled=True

time: 370 us -> 406 us (1.097)
  waiting for transfers between devices: 220 us -> 243 us
  starting transfers between devices: 0.15 us -> 8.59 us
  local copies, waits for them, and re-layouts: 48.2 us -> 52.7 us
    all_gather x1, waiting for transfers between devices: 17 us -> 79.1 us  [verify(): lax.all_gather(w_query, 'row', axis=0, tiled=True)]
    all_gather x1 -> x0, waiting for transfers between devices: 39.6 us -> none  [verify(): lax.all_gather(w_out, 'row', axis=1, tiled=True)]
    all_to_all x0 -> x1, starting transfers between devices: none -> 8.47 us  [verify(): lax.all_to_all(jnp.stack([w_out] * lax.axis_size('row')), 'row', 0, 0)]
    another operation x0 -> x1, local copies, waits for them, and re-layouts: none -> 4.45 us  [verify(): jnp.stack([w_out] * lax.axis_size('row'))]
    unnamed x6 -> x5, waiting for transfers between devices: 64.2 us -> 63.7 us
  transfers between devices with their start and end apart: 5 -> 5, of which waited for: 5 -> 4; matrix products, arithmetic and copies ran while one was open for 27% -> 26% of each run, Pallas kernels for 0% -> 0%
where the time goes in v1:
time: 406 us; the launch traced here: 405 us
  waiting for transfers between devices  243 us (60%)
  matrix products  58.3 us (14%)
  local copies, waits for them, and re-layouts  52.7 us (13%)
  other arithmetic  29.3 us (7%)
  between operations  13.3 us (3%)
  starting transfers between devices  8.59 us (2%)
    all_gather x1, waiting for transfers between devices, verify(): lax.all_gather(w_query, 'row', axis=0, tiled=True)  79.1 us
    unnamed x5, waiting for transfers between devices  63.7 us
    all_gather x1, waiting for transfers between devices, verify(): lax.all_gather(w_key, 'row', axis=0, tiled=True)  51.1 us
    all_gather x1, waiting for transfers between devices, verify(): lax.all_gather(w_value, 'row', axis=0, tiled=True)  48.9 us
    gather x1, local copies, waits for them, and re-layouts, prepare(): jnp.take(embed_table, group_ids, axis=0).astype(jnp.float32)  21.8 us
    unnamed x16, local copies, waits for them, and re-layouts  18.5 us
    dot_general x1, matrix products, verify(): jnp.dot(mixed, jnp.concatenate(lax.all_to_all(jnp.stack([w_out] * lax.axi...  14 us
    dot_general x1, matrix products, verify(): jnp.dot(flat, lax.all_gather(w_value, 'row', axis=0, tiled=True), preferr...  12.9 us
  transfers between devices with their start and end apart: 5, of which 4 were waited for; matrix products, arithmetic and copies ran while one was open for 26% of the time, Pallas kernels for 0%

profile of v1, /device:TPU:1, one launch (start us, length us, event | category | flops | bytes accessed | tf_op | source)
XLA Modules:
  0.0 404.8 jit_solution(9972556266043003958)
XLA Ops:
  6.5 0.7 all-gather.6.cloned.1.call-update
  7.3 0.7 all-gather.8.cloned.1.call-update
  8.1 0.7 all-gather.4.cloned.1.call-update
  8.7 4.4 %stack.2 = bf16[16,640,320]{1,2,0:T(8,128)(2,1)} broadcast(bf16[640,320]{0,1:T(8,128)(2,1)} %param.19), dimensions={1,2} | broadcast | bytes 6963200 | tf_op jit(solution)/shard_map/stack | solution.py:72
  13.2 8.5 %all-to-all-start = ((bf16[16,640,320]{1,2,0:T(8,128)(2,1)}), bf16[16,640,320]{1,2,0:T(8,128)(2,1)}, u32[]{:S(2)}, u32[]{:S(2)}) async-start(bf16[16,640,320]{1,2,0:T(8,128)(2,1)} %stack.2), calls=%async_computation | async-start | bytes 13107200 | tf_op jit(solution)/shard_map/all_to_all | solution.py:72
  21.7 1.6 convert_element_type.57
  23.4 21.8 %gather_fusion = bf16[1024,5120]{1,0:T(8,128)(2,1)} fusion(bf16[512,5120]{1,0:T(8,128)(2,1)} %param.13, s32[1024]{0:T(1024)S(1)} %bitcast_clamp_fusion), kind=kCustom, calls=%fused_computation | custom fusion | bytes 20975616 | tf_op jit(solution)/shard_map/jit(_take)/gather | solution.py:11
  45.3 11.0 %add_convert_fusion = bf16[8,128,5120]{2,1,0:T(8,128)(2,1)} fusion(f32[128,5120]{1,0:T(8,128)S(1)} %convert_element_type.57, bf16[8,128,5120]{2,1,0:T(8,128)(2,1)} %bitcast.31, pred[8,128]{1,0:T(8,128)(4,1)S(1)} %compare_and_fusion), kind=kLoop, calls=%fused_computation.7 | loop fusion | flops 20971520 | bytes 23593984 | tf_op jit(solution)/shard_map/convert_element_type | solution.py:14
  56.3 0.6 dynamic_slice.7
  56.9 6.3 %fusion.1 = f32[8,128]{1,0:T(8,128)S(1)} fusion(bf16[8,128,5120]{2,1,0:T(8,128)(2,1)} %add_convert_fusion), kind=kLoop, calls=%fused_computation.4 | loop fusion | flops 15727616 | bytes 10489856 | tf_op jit(solution)/shard_map/reduce_sum | solution.py:16
  63.2 0.7 copy-done
  63.9 5.9 %fusion.3 = bf16[8,128,5120]{2,1,0:T(8,128)(2,1)} fusion(bf16[8,128,5120]{2,1,0:T(8,128)(2,1)S(1)} %copy-done, f32[5120]{0:T(1024)S(1)} %copy-done.3, f32[8,128]{1,0:T(8,128)S(1)} %add_rsqrt_fusion), kind=kLoop, calls=%fused_computation.6 | loop fusion | flops 20971520 | bytes 20996096 | tf_op jit(solution)/shard_map/convert_element_type | solution.py:17
  69.9 0.6 iota_compare_fusion.1
  70.6 79.1 %all-gather.6.cloned.1.call-done = bf16[5120,640]{1,0:T(8,128)(2,1)} async-done(((bf16[320,640]{1,0:T(8,128)(2,1)}), bf16[5120,640]{1,0:T(8,128)(2,1)}) %all-gather.6.cloned.1.call-update) | async-done | bytes 6553616 | tf_op jit(solution)/shard_map/all_gather | solution.py:55
  149.7 12.9 %convolution_convert_fusion.3 = bf16[1024,640]{1,0:T(8,128)(2,1)S(1)} fusion(bf16[1024,5120]{1,0:T(8,128)(2,1)} %bitcast.33, bf16[5120,640]{1,0:T(8,128)(2,1)} %all-gather.6.cloned.1.call-done), kind=kOutput, calls=%fused_computation.16 | convolution fusion | flops 6711541760 | bytes 18350080 | tf_op jit(solution)/shard_map/dot_general | solution.py:54
  162.6 1.5 reshape.113
  164.1 51.1 %all-gather.8.cloned.1.call-done = bf16[5120,640]{1,0:T(8,128)(2,1)} async-done(((bf16[320,640]{1,0:T(8,128)(2,1)}), bf16[5120,640]{1,0:T(8,128)(2,1)}) %all-gather.8.cloned.1.call-update) | async-done | bytes 6553616 | tf_op jit(solution)/shard_map/all_gather | solution.py:58
  215.1 12.9 %convolution_convert_fusion.2 = bf16[1024,640]{1,0:T(8,128)(2,1)S(1)} fusion(bf16[1024,5120]{1,0:T(8,128)(2,1)} %bitcast.34, bf16[5120,640]{1,0:T(8,128)(2,1)} %all-gather.8.cloned.1.call-done), kind=kOutput, calls=%fused_computation.15 | convolution fusion | flops 6711541760 | bytes 18350080 | tf_op jit(solution)/shard_map/dot_general | solution.py:57
  228.0 2.5 reshape.114
  230.5 48.9 %all-gather.4.cloned.1.call-done = bf16[5120,640]{1,0:T(8,128)(2,1)} async-done(((bf16[320,640]{1,0:T(8,128)(2,1)}), bf16[5120,640]{1,0:T(8,128)(2,1)}) %all-gather.4.cloned.1.call-update) | async-done | bytes 6553616 | tf_op jit(solution)/shard_map/all_gather | solution.py:61
  279.4 12.9 %convolution_convert_fusion.4 = bf16[1024,640]{1,0:T(8,128)(2,1)S(1)} fusion(bf16[1024,5120]{1,0:T(8,128)(2,1)} %bitcast.35, bf16[5120,640]{1,0:T(8,128)(2,1)} %all-gather.4.cloned.1.call-done), kind=kOutput, calls=%fused_computation.17 | convolution fusion | flops 6711541760 | bytes 18350080 | tf_op jit(solution)/shard_map/dot_general | solution.py:60
  292.3 2.4 reshape.112
  294.8 2.6 fusion.8
  297.4 1.5 copy-done.1
  298.9 0.8 fusion.23
  299.9 3.0 fusion.5
  303.0 0.9 copy.31
  303.9 14.0 %convolution_convert_fusion = bf16[1024,5120]{1,0:T(8,128)(2,1)} fusion(bf16[640,5120]{0,1:T(8,128)(2,1)} %bitcast.6, bf16[80,8,8,128]{3,2,1,0:T(8,128)(2,1)S(1)} %bitcast.37), kind=kOutput, calls=%fused_computation.8 | convolution fusion | flops 6716129280 | bytes 18350080 | tf_op jit(solution)/shard_map/dot_general | solution.py:69
  317.8 14.4 %copy.39 = bf16[1024,5120]{0,1:T(8,128)(2,1)} copy(bf16[1024,5120]{1,0:T(8,128)(2,1)} %convolution_convert_fusion) | data formatting | bytes 20971520
  332.2 61.6 %reduce-scatter.4.cloned.1.call-done = bf16[640,1024]{1,0:T(8,128)(2,1)} async-done(((bf16[5120,1024]{1,0:T(8,128)(2,1)}), bf16[640,1024]{1,0:T(8,128)(2,1)}) %reduce-scatter.4.cloned.1.call-update) | async-done | bytes 1310736
  393.8 1.7 copy.40
  395.5 2.8 multiply_convert_fusion
  (22 shorter events, 0.4 us)
Async XLA Ops:
  6.5 143.1 %all-gather.6.cloned.1.call-start = ((), (), s32[]{:S(2)}) async-start(), calls=%async_computation.3 | async-start | bytes 6963200 | tf_op jit(solution)/shard_map/all_gather | solution.py:55
  7.3 207.9 %all-gather.8.cloned.1.call-start = ((), (), s32[]{:S(2)}) async-start(), calls=%async_computation.4 | async-start | bytes 6963200 | tf_op jit(solution)/shard_map/all_gather | solution.py:58
  8.0 271.4 %all-gather.4.cloned.1.call-start = ((), (), s32[]{:S(2)}) async-start(), calls=%async_computation.2 | async-start | bytes 6963200 | tf_op jit(solution)/shard_map/all_gather | solution.py:61
  13.2 290.7 %all-to-all-start = ((bf16[16,640,320]{1,2,0:T(8,128)(2,1)}), bf16[16,640,320]{1,2,0:T(8,128)(2,1)}, u32[]{:S(2)}, u32[]{:S(2)}) async-start(bf16[16,640,320]{1,2,0:T(8,128)(2,1)} %stack.2), calls=%async_computation | async-start | bytes 13107200 | tf_op jit(solution)/shard_map/all_to_all | solution.py:72
  21.7 1.7 copy-start.4
  21.7 372.1 %reduce-scatter.4.cloned.1.call-start = ((), (), s32[]{:S(2)}) async-start(), calls=%async_computation.5 | async-start | bytes 11796480
  45.2 11.0 %copy-start.6 = (s32[16]{0:T(128)S(1)}, s32[16]{0:T(128)}, u32[]{:S(2)}) copy-start(s32[16]{0:T(128)} %param.12) | copy-start | bytes 196
  45.2 17.9 %copy-start.3 = (f32[5120]{0:T(1024)S(1)}, f32[5120]{0:T(1024)}, u32[]{:S(2)}) copy-start(f32[5120]{0:T(1024)} %param.15) | copy-start | bytes 61444
  56.9 7.1 %copy-start = (bf16[8,128,5120]{2,1,0:T(8,128)(2,1)S(1)}, bf16[8,128,5120]{2,1,0:T(8,128)(2,1)}, u32[]{:S(2)}) copy-start(bf16[8,128,5120]{2,1,0:T(8,128)(2,1)} %add_convert_fusion) | copy-start | bytes 31457284
  63.9 6.6 %copy-start.5 = (s32[8]{0:T(128)S(1)}, s32[8]{0:T(128)}, u32[]{:S(2)}) copy-start(s32[8]{0:T(128)} %param.11) | copy-start | bytes 100
  297.4 1.5 copy-start.1
  297.4 2.5 copy-start.2
Sparse Core Ops, SparseCore 0:
  9.5 140.1 all-gather.5
  151.8 63.2 all-gather.7
  217.3 62.1 all-gather.3
  332.4 61.3 reduce-scatter.3
